TPU v7x, 256 devices: a whole 4x4x8 slice. The times are simulated.
256 devices in a mesh: seq: 16 (over x_hi, y, core), head: 16 (over x_lo, z).
Axes of the slice: x: 4 (x_hi: 2, x_lo: 2; x = x_hi * 2 + x_lo), y: 4, z: 8, core: 2. Of those that a mesh axis runs over, the one named last changes fastest.
Arguments:
- grad_out: bfloat16 [4096, 8192], P('seq', 'head'), may hold values from -6 to 6
- out_weight: bfloat16 [16384, 8192], P('head', 'seq'), may hold values from -0.046875 to 0.046875
- ssm_input: bfloat16 [4096, 16384], P('seq', 'head'), may hold values from -6 to 6
- step_size: float32 [4096, 128], P('seq', 'head'), may hold values from 0.02 to 0.2
- log_decay: float32 [4096, 128], P('seq', 'head'), may hold values from -1 to 0, as said below
- b_in: bfloat16 [4096, 256], P('seq'), may hold values from -1.5 to 1.5
- c_in: bfloat16 [4096, 256], P('seq'), may hold values from -1.5 to 1.5
- skip: float32 [128], P('head'), may hold values from 0.5 to 1.5
Outputs:
- grad_input: bfloat16 [4096, 16384], P('seq', 'head')
- grad_step: float32 [4096, 128], P('seq', 'head')
- grad_decay: float32 [4096, 128], P('seq', 'head')
- grad_b: float32 [4096, 256], P('seq')
- grad_c: float32 [4096, 256], P('seq')
Inputs may be any that keep to these rules, and one draw needn't show every extreme that they name: `log_decay`: every entry is negative.
All inputs are finite; a program needn't handle non-finite values.
Results may differ from a plain program's by a relative error of at most 0.0049.
Values may be sent and summed in bfloat16 or wider, within the bound.
A program may use at most 64 MiB of HBM per device.

v0:
```python
import jax
import jax.numpy as jnp
from jax import lax
from jax.sharding import PartitionSpec as P

HIGH = lax.Precision.HIGHEST


def entering(part, axis, combine, identity, reverse):
    count = lax.axis_size(axis)
    place = lax.axis_index(axis)
    ahead = count - 1 - place if reverse else place
    gathered = jax.tree.map(lambda a: lax.all_gather(a, axis), part)
    state = jax.tree.map(lambda a, e: jnp.zeros_like(a) + jnp.asarray(e, a.dtype), part, identity)

    def one(hop, state):
        source = count - 1 - hop if reverse else hop
        return combine(
            state, jax.tree.map(lambda a: lax.dynamic_index_in_dim(a, source, 0, False), gathered)
        )

    return lax.fori_loop(0, ahead, one, state)


def inner_terms(inputs, strides, running, b_rows, c_rows, skips):
    span = inputs.shape[0]
    row_pos = lax.broadcasted_iota(jnp.int32, (span, span), 0)
    col_pos = lax.broadcasted_iota(jnp.int32, (span, span), 1)
    causal = row_pos >= col_pos
    running_t = running.T
    gaps = running_t[:, :, None] - running_t[:, None, :]
    weights = jnp.exp(jnp.where(causal[None], gaps, -jnp.inf)) * strides.T[:, None, :]
    intersection = jnp.dot(c_rows, b_rows.T, precision=HIGH)
    mixed_sum = jnp.einsum("hts,shp->thp", weights * intersection[None], inputs, precision=HIGH)
    return mixed_sum + skips[None, :, None] * inputs


def carried(c_rows, running, carried_state):
    readout = jnp.einsum("tn,hpn->thp", c_rows, carried_state, precision=HIGH)
    return readout * jnp.exp(running)[:, :, None]


def closing(inputs, strides, b_rows, running, carried_state):
    block_end = running[-1]
    input_scale = strides * jnp.exp(block_end[None, :] - running)
    fresh = jnp.einsum("thp,tn->hpn", inputs * input_scale[:, :, None], b_rows, precision=HIGH)
    return jnp.exp(block_end)[:, None, None] * carried_state + fresh


def block_forward(inputs, strides, decays, b_rows, c_rows, skips, carried_state):
    running = jnp.cumsum(decays, axis=0)
    outputs = inner_terms(inputs, strides, running, b_rows, c_rows, skips) + carried(
        c_rows, running, carried_state
    )
    return (outputs, closing(inputs, strides, b_rows, running, carried_state))


def compose(first_part, second_part):
    return (
        first_part[0] * second_part[0],
        second_part[0][:, None, None] * first_part[1] + second_part[1],
    )


def local(grad_out, out_weight, ssm_input, step_size, log_decay, b_in, c_in, skip):
    full_grad = lax.all_gather(grad_out, "head", axis=1, tiled=True)
    span = ssm_input.shape[0]
    head_count = step_size.shape[1]
    head_width = ssm_input.shape[1] // head_count
    state_count = b_in.shape[1]
    grad_y = lax.dot_general(
        full_grad,
        lax.all_gather(out_weight, "seq", axis=1, tiled=True),
        (((1,), (1,)), ((), ())),
        preferred_element_type=jnp.float32,
    ).astype(jnp.bfloat16)
    inputs = ssm_input.astype(jnp.float32).reshape(span, head_count, head_width)
    upstream = grad_y.astype(jnp.float32).reshape(span, head_count, head_width)
    b_float = b_in.astype(jnp.float32)
    c_float = c_in.astype(jnp.float32)
    zero_state = jnp.zeros((head_count, head_width, state_count), jnp.float32)
    running = jnp.cumsum(log_decay, axis=0)
    block_decay = jnp.exp(running[-1])
    local_states = closing(inputs, step_size, b_float, running, zero_state)
    local_grads = jnp.einsum(
        "thp,tn->hpn", upstream * jnp.exp(running)[:, :, None], c_float, precision=HIGH
    )
    identity = (jnp.ones((head_count,), jnp.float32), jnp.zeros_like(zero_state))
    incoming = entering((block_decay, local_states), "seq", compose, identity, False)[1]
    outgoing = entering((block_decay, local_grads), "seq", compose, identity, True)[1]

    def forward_full(inputs_v, strides_v, decays_v, b_rows, c_rows):
        return block_forward(inputs_v, strides_v, decays_v, b_rows, c_rows, skip, incoming)

    pull_full = jax.vjp(forward_full, inputs, step_size, log_decay, b_float, c_float)[1]
    gradients = pull_full((upstream, outgoing))
    grad_b, grad_c = lax.psum((gradients[3], gradients[4]), "head")
    grad_input = gradients[0].reshape(span, head_count * head_width).astype(jnp.bfloat16)
    return (grad_input, gradients[1], gradients[2], grad_b, grad_c)


def solution(mesh):
    in_specs = (
        P("seq", "head"),
        P("head", "seq"),
        P("seq", "head"),
        P("seq", "head"),
        P("seq", "head"),
        P("seq", None),
        P("seq", None),
        P("head"),
    )
    out_specs = (
        P("seq", "head"),
        P("seq", "head"),
        P("seq", "head"),
        P("seq", None),
        P("seq", None),
    )
    return jax.shard_map(local, mesh=mesh, in_specs=in_specs, out_specs=out_specs, check_vma=False)
```

profile of v0, /device:TPU:8, one launch (start us, length us, event | category | flops | bytes accessed | tf_op | source)
XLA Modules:
  0.0 649.4 jit_solution(1202185131992663605)
XLA Ops:
  10.2 79.4 %all-gather.8.cloned.1.call-done = bf16[256,8192]{1,0:T(8,128)(2,1)} async-done(((bf16[256,512]{1,0:T(8,128)(2,1)}), bf16[256,8192]{1,0:T(8,128)(2,1)}) %all-gather.8.cloned.1.call-update) | async-done | bytes 4194320 | tf_op jit(solution)/shard_map/all_gather | solution.py:66
  89.6 122.1 %all-gather.10.cloned.1.call-done = bf16[1024,8192]{1,0:T(8,128)(2,1)} async-done(((bf16[1024,512]{1,0:T(8,128)(2,1)}), bf16[1024,8192]{1,0:T(8,128)(2,1)}) %all-gather.10.cloned.1.call-update) | async-done | bytes 16777232 | tf_op jit(solution)/shard_map/all_gather | solution.py:73
  211.7 11.6 %convolution_convert_fusion = bf16[256,1024]{1,0:T(8,128)(2,1)S(1)} fusion(bf16[256,8192]{1,0:T(8,128)(2,1)} %all-gather.8.cloned.1.call-done, bf16[1024,8192]{1,0:T(8,128)(2,1)} %all-gather.10.cloned.1.call-done), kind=kOutput, calls=%fused_computation.22 | convolution fusion | flops 4295229440 | bytes 21495808 | tf_op jit(solution)/shard_map/dot_general | solution.py:71
  224.2 1.7 fusion.15
  226.3 21.3 %all-gather.2 = f32[16,1,8]{2,1,0:T(1,128)S(1)} all-gather(f32[1,1,8]{2,1,0:T(1,128)S(1)} %bitcast.129), channel_id=1, replica_groups=mesh['seq'=16,'head'=16] {'seq'}, dimensions={0}, use_global_device_ids=true | all-gather | bytes 544 | tf_op jit(solution)/shard_map/all_gather | solution.py:13
  248.5 1.6 fusion.18
  250.1 88.0 %all-gather.12.cloned.1.call-done = f32[128,128,256]{2,1,0:T(8,128)} async-done(((f32[8,128,256]{2,1,0:T(8,128)}), f32[128,128,256]{2,1,0:T(8,128)}) %all-gather.12.cloned.1.call-update) | async-done | bytes 16777232 | tf_op jit(solution)/shard_map/all_gather | solution.py:13
  338.2 20.5 %while.26 = (s32[]{:T(128)}, f32[8,128,256]{2,1,0:T(8,128)S(1)}, s32[]{:T(128)}, f32[16,8]{1,0:T(8,128)S(1)}, f32[16,8,128,256]{3,2,1,0:T(8,128)}, /*index=5*/s32[]{:T(128)}, s32[]{:T(128)}, s32[]{:T(128)}, s32[]{:T(128)}) while((s32[]{:T(128)}, f32[8,128,256]{2,1,0:T(8,128)S(1)}, s32[]{:T(128)}, f32[16,8]{1,0:T(8,128)S(1)}, ...), condition=%wide.region_3.4_spmd, body=%wide.region_2.3_spmd.sunk | while | flops 524294 | bytes 3145979 | solution.py:22
  338.2 1.5 bitcast_add_fusion.6
  350.8 1.5 bitcast_add_fusion.6
  354.0 1.5 bitcast_add_fusion.6
  357.1 1.5 bitcast_add_fusion.6
  358.7 1.7 fusion.21
  361.7 1.7 convolution_add_fusion
  363.6 3.8 fusion.10
  367.4 2.0 copy.70
  369.5 1.8 fusion.20
  372.4 104.9 %all-gather.14.cloned.1.call-done = f32[128,128,256]{2,1,0:T(8,128)} async-done(((f32[8,128,256]{2,1,0:T(8,128)}), f32[128,128,256]{2,1,0:T(8,128)}) %all-gather.14.cloned.1.call-update) | async-done | bytes 16777232 | tf_op jit(solution)/shard_map/all_gather | solution.py:13
  477.4 3.2 while.27
  481.5 1.8 fusion.19
  484.5 2.5 reduce-window.16
  487.8 151.7 %all-reduce.4.cloned.1.call-done = (f32[256,256]{1,0:T(8,128)}, f32[256,256]{1,0:T(8,128)}) async-done(((f32[256,256]{1,0:T(8,128)}, f32[256,256]{1,0:T(8,128)}), (f32[256,256]{1,0:T(8,128)}, f32[256,256]{1,0:T(8,128)})) %all-reduce.4.cloned.1.call-update) | async-done | bytes 524304 | tf_op jit(solution)/shard_map/psum | solution.py:97
  639.5 1.7 copy.107
  641.2 1.7 copy.108
  (80 shorter events, 28.0 us)
Async XLA Ops:
  7.2 241.1 %copy-start = (bf16[256,256]{1,0:T(8,128)(2,1)S(1)}, bf16[256,256]{1,0:T(8,128)(2,1)}, u32[]{:S(2)}) copy-start(bf16[256,256]{1,0:T(8,128)(2,1)} %param.17) | copy-start | bytes 393220
  7.2 82.4 %all-gather.8.cloned.1.call-start = ((), (), s32[]{:S(2)}) async-start(), calls=%async_computation | async-start | bytes 4456448 | tf_op jit(solution)/shard_map/all_gather | solution.py:66
  7.9 203.8 %all-gather.10.cloned.1.call-start = ((), (), s32[]{:S(2)}) async-start(), calls=%async_computation.1 | async-start | bytes 17825792 | tf_op jit(solution)/shard_map/all_gather | solution.py:73
  8.7 329.4 %all-gather.12.cloned.1.call-start = ((), (), s32[]{:S(2)}) async-start(), calls=%async_computation.2 | async-start | bytes 17825792 | tf_op jit(solution)/shard_map/all_gather | solution.py:13
  223.2 0.9 copy-start.1
  223.4 2.5 copy-start.2
  224.2 24.3 %copy-start.3 = (f32[256,8]{0,1:T(8,128)S(1)}, f32[256,8]{0,1:T(8,128)}, u32[]{:S(2)}) copy-start(f32[256,8]{0,1:T(8,128)} %param.15) | copy-start | bytes 24580
  225.8 251.5 %all-gather.14.cloned.1.call-start = ((), (), s32[]{:S(2)}) async-start(), calls=%async_computation.3 | async-start | bytes 17825792 | tf_op jit(solution)/shard_map/all_gather | solution.py:13
  226.3 23.8 %copy-start.4 = (f32[8]{0:T(128)}, f32[8]{0:T(128)S(1)}, u32[]{:S(2)}) copy-start(f32[8]{0:T(128)S(1)} %get-tuple-element.199) | copy-start | bytes 100
  358.7 1.7 copy-start.5
  358.7 3.0 copy-start.7
  363.4 276.2 %all-reduce.4.cloned.1.call-start = ((), (), s32[]{:S(2)}) async-start(), calls=%async_computation.4 | async-start | bytes 1048576 | tf_op jit(solution)/shard_map/psum | solution.py:97
  363.6 5.8 copy-start.6
Sparse Core Ops, SparseCore 0:
  9.8 79.7 all-gather.7
  92.2 119.4 all-gather.9
  226.0 112.0 all-gather.11
  363.5 113.8 all-gather.13
  484.6 154.9 all-reduce.3
where the time goes:
time: 650 us; the launch traced here: 649 us
  waiting for transfers between devices  548 us (84%)
  other arithmetic  29.9 us (5%)
  matrix products  28.4 us (4%)
  blocking collectives  21.3 us (3%)
  between operations  14 us (2%)
  local copies, waits for them, and re-layouts  7.42 us (1%)
    all_gather x2, waiting for transfers between devices, entering(): gathered = jax.tree.map(lambda a: lax.all_gather(a, axis), part)  193 us
    psum x1, waiting for transfers between devices, local(): grad_b, grad_c = lax.psum((gradients[3], gradients[4]), 'head')  152 us
    all_gather x1, waiting for transfers between devices, local(): lax.all_gather(out_weight, 'seq', axis=1, tiled=True)  122 us
    all_gather x1, waiting for transfers between devices, local(): full_grad = lax.all_gather(grad_out, 'head', axis=1, tiled=True)  79.4 us
    add x15, other arithmetic, compose(): second_part[0][:, None, None] * first_part[1] + second_part[1]  23 us
    all_gather x1, blocking collectives, entering(): gathered = jax.tree.map(lambda a: lax.all_gather(a, axis), part)  21.3 us
  transfers between devices with their start and end apart: 5, of which 5 were waited for; matrix products, arithmetic and copies ran while one was open for 3% of the time, Pallas kernels for 0%

commit v1 on v0

--- a/solution.py
+++ b/solution.py
@@ -4,6 +4,11 @@
 from jax.sharding import PartitionSpec as P
 
 HIGH = lax.Precision.HIGHEST
+
+
+def swapped_in(x, mesh_axis, dim):
+    outgoing = jnp.stack([x] * lax.axis_size(mesh_axis))
+    return jnp.concatenate(lax.all_to_all(outgoing, mesh_axis, 0, 0), axis=dim)
 
 
 def entering(part, axis, combine, identity, reverse):
@@ -63,7 +68,7 @@
 
 
 def local(grad_out, out_weight, ssm_input, step_size, log_decay, b_in, c_in, skip):
-    full_grad = lax.all_gather(grad_out, "head", axis=1, tiled=True)
+    full_grad = swapped_in(grad_out, "head", 1)
     span = ssm_input.shape[0]
     head_count = step_size.shape[1]
     head_width = ssm_input.shape[1] // head_count

time: 650 us -> 606 us (0.932)
  waiting for transfers between devices: 548 us -> 491 us
  starting transfers between devices: 0.38 us -> 10 us
    all_to_all x0 -> x1, waiting for transfers between devices: none -> 94.4 us  [swapped_in(): return jnp.concatenate(lax.all_to_all(outgoing, mesh_axis, 0, 0), axis=dim)]
    all_gather x1 -> x0, waiting for transfers between devices: 79.4 us -> none  [local(): full_grad = lax.all_gather(grad_out, 'head', axis=1, tiled=True)]
    all_gather x1, waiting for transfers between devices: 122 us -> 45.6 us  [local(): lax.all_gather(out_weight, 'seq', axis=1, tiled=True)]
    all_to_all x0 -> x1, starting transfers between devices: none -> 9.68 us  [swapped_in(): return jnp.concatenate(lax.all_to_all(outgoing, mesh_axis, 0, 0), axis=dim)]
where the time goes in v1:
time: 606 us; the launch traced here: 605 us
  waiting for transfers between devices  491 us (81%)
  other arithmetic  29.2 us (5%)
  matrix products  28.5 us (5%)
  blocking collectives  21.4 us (4%)
  between operations  14 us (2%)
  local copies, waits for them, and re-layouts  10.9 us (2%)
  starting transfers between devices  10 us (2%)
    all_gather x2, waiting for transfers between devices, entering(): gathered = jax.tree.map(lambda a: lax.all_gather(a, axis), part)  198 us
    psum x1, waiting for transfers between devices, local(): grad_b, grad_c = lax.psum((gradients[3], gradients[4]), 'head')  152 us
    all_to_all x1, waiting for transfers between devices, swapped_in(): return jnp.concatenate(lax.all_to_all(outgoing, mesh_axis, 0, 0), axis=dim)  94.4 us
    all_gather x1, waiting for transfers between devices, local(): lax.all_gather(out_weight, 'seq', axis=1, tiled=True)  45.6 us
    add x15, other arithmetic, compose(): second_part[0][:, None, None] * first_part[1] + second_part[1]  23 us
    all_gather x1, blocking collectives, entering(): gathered = jax.tree.map(lambda a: lax.all_gather(a, axis), part)  21.4 us
  transfers between devices with their start and end apart: 5, of which 5 were waited for; matrix products, arithmetic and copies ran while one was open for 3% of the time, Pallas kernels for 0%

profile of v1, /device:TPU:8, one launch (start us, length us, event | category | flops | bytes accessed | tf_op | source)
XLA Modules:
  0.0 605.3 jit_solution(14814258555150777460)
XLA Ops:
  9.0 2.4 stack.2
  11.4 9.7 %all-to-all-start = ((bf16[16,256,512]{1,2,0:T(8,128)(2,1)}), bf16[16,256,512]{1,2,0:T(8,128)(2,1)}, u32[]{:S(2)}, u32[]{:S(2)}) async-start(bf16[16,256,512]{1,2,0:T(8,128)(2,1)} %stack.2), calls=%async_computation | async-start | bytes 8388608 | tf_op jit(solution)/shard_map/all_to_all | solution.py:11
  22.0 94.4 %all-to-all-done = bf16[16,256,512]{1,2,0:T(8,128)(2,1)} async-done(((bf16[16,256,512]{1,2,0:T(8,128)(2,1)}), bf16[16,256,512]{1,2,0:T(8,128)(2,1)}, u32[]{:S(2)}, u32[]{:S(2)}) %all-to-all-start) | async-done | bytes 4194336 | tf_op jit(solution)/shard_map/all_to_all | solution.py:11
  116.4 45.6 %all-gather.7.cloned.1.call-done = bf16[1024,8192]{1,0:T(8,128)(2,1)} async-done(((bf16[1024,512]{1,0:T(8,128)(2,1)}), bf16[1024,8192]{1,0:T(8,128)(2,1)}) %all-gather.7.cloned.1.call-update) | async-done | bytes 16777232 | tf_op jit(solution)/shard_map/all_gather | solution.py:78
  162.0 11.6 %convolution_convert_fusion = bf16[256,1024]{1,0:T(8,128)(2,1)S(1)} fusion(bf16[256,8192]{0,1:T(8,128)(2,1)} %bitcast.11, bf16[1024,8192]{1,0:T(8,128)(2,1)} %all-gather.7.cloned.1.call-done), kind=kOutput, calls=%fused_computation.22 | convolution fusion | flops 4295229440 | bytes 21495808 | tf_op jit(solution)/shard_map/dot_general | solution.py:76
  174.5 1.7 fusion.15
  176.7 21.4 %all-gather.2 = f32[16,1,8]{2,1,0:T(1,128)S(1)} all-gather(f32[1,1,8]{2,1,0:T(1,128)S(1)} %bitcast.132), channel_id=1, replica_groups=mesh['seq'=16,'head'=16] {'seq'}, dimensions={0}, use_global_device_ids=true | all-gather | bytes 544 | tf_op jit(solution)/shard_map/all_gather | solution.py:18
  198.9 1.6 fusion.18
  200.5 93.5 %all-gather.9.cloned.1.call-done = f32[128,128,256]{2,1,0:T(8,128)} async-done(((f32[8,128,256]{2,1,0:T(8,128)}), f32[128,128,256]{2,1,0:T(8,128)}) %all-gather.9.cloned.1.call-update) | async-done | bytes 16777232 | tf_op jit(solution)/shard_map/all_gather | solution.py:18
  294.1 20.5 %while.26 = (s32[]{:T(128)}, f32[8,128,256]{2,1,0:T(8,128)S(1)}, s32[]{:T(128)}, f32[16,8]{1,0:T(8,128)S(1)}, f32[16,8,128,256]{3,2,1,0:T(8,128)}, /*index=5*/s32[]{:T(128)}, s32[]{:T(128)}, s32[]{:T(128)}, s32[]{:T(128)}) while((s32[]{:T(128)}, f32[8,128,256]{2,1,0:T(8,128)S(1)}, s32[]{:T(128)}, f32[16,8]{1,0:T(8,128)S(1)}, ...), condition=%wide.region_3.4_spmd, body=%wide.region_2.3_spmd.sunk | while | flops 524294 | bytes 3145979 | solution.py:27
  294.1 1.5 bitcast_add_fusion.6
  297.3 1.5 bitcast_add_fusion.6
  314.6 1.7 fusion.21
  317.6 1.7 convolution_add_fusion
  319.5 3.8 fusion.10
  323.3 2.0 copy.73
  325.4 1.8 fusion.20
  328.3 104.9 %all-gather.11.cloned.1.call-done = f32[128,128,256]{2,1,0:T(8,128)} async-done(((f32[8,128,256]{2,1,0:T(8,128)}), f32[128,128,256]{2,1,0:T(8,128)}) %all-gather.11.cloned.1.call-update) | async-done | bytes 16777232 | tf_op jit(solution)/shard_map/all_gather | solution.py:18
  433.4 3.2 while.27
  437.4 1.8 fusion.19
  440.4 2.5 reduce-window.16
  443.7 151.7 %all-reduce.4.cloned.1.call-done = (f32[256,256]{1,0:T(8,128)}, f32[256,256]{1,0:T(8,128)}) async-done(((f32[256,256]{1,0:T(8,128)}, f32[256,256]{1,0:T(8,128)}), (f32[256,256]{1,0:T(8,128)}, f32[256,256]{1,0:T(8,128)})) %all-reduce.4.cloned.1.call-update) | async-done | bytes 524304 | tf_op jit(solution)/shard_map/psum | solution.py:102
  595.4 1.7 copy.110
  597.1 1.7 copy.111
  (83 shorter events, 30.8 us)
Async XLA Ops:
  7.2 191.5 %copy-start = (bf16[256,256]{1,0:T(8,128)(2,1)S(1)}, bf16[256,256]{1,0:T(8,128)(2,1)}, u32[]{:S(2)}) copy-start(bf16[256,256]{1,0:T(8,128)(2,1)} %param.17) | copy-start | bytes 393220
  7.2 154.8 %all-gather.7.cloned.1.call-start = ((), (), s32[]{:S(2)}) async-start(), calls=%async_computation.1 | async-start | bytes 17825792 | tf_op jit(solution)/shard_map/all_gather | solution.py:78
  11.4 9.7 %copy-start.4 = (f32[256,8]{0,1:T(8,128)S(1)}, f32[256,8]{0,1:T(8,128)}, u32[]{:S(2)}) copy-start(f32[256,8]{0,1:T(8,128)} %param.16) | copy-start | bytes 24580
  11.4 105.0 %all-to-all-start = ((bf16[16,256,512]{1,2,0:T(8,128)(2,1)}), bf16[16,256,512]{1,2,0:T(8,128)(2,1)}, u32[]{:S(2)}, u32[]{:S(2)}) async-start(bf16[16,256,512]{1,2,0:T(8,128)(2,1)} %stack.2), calls=%async_computation | async-start | bytes 8388608 | tf_op jit(solution)/shard_map/all_to_all | solution.py:11
  21.1 272.9 %all-gather.9.cloned.1.call-start = ((), (), s32[]{:S(2)}) async-start(), calls=%async_computation.2 | async-start | bytes 17825792 | tf_op jit(solution)/shard_map/all_gather | solution.py:18
  173.6 0.9 copy-start.1
  173.7 2.5 copy-start.2
  174.5 24.4 %copy-start.3 = (f32[256,8]{0,1:T(8,128)S(1)}, f32[256,8]{0,1:T(8,128)}, u32[]{:S(2)}) copy-start(f32[256,8]{0,1:T(8,128)} %param.15) | copy-start | bytes 24580
  176.2 257.1 %all-gather.11.cloned.1.call-start = ((), (), s32[]{:S(2)}) async-start(), calls=%async_computation.3 | async-start | bytes 17825792 | tf_op jit(solution)/shard_map/all_gather | solution.py:18
  176.7 23.8 %copy-start.5 = (f32[8]{0:T(128)}, f32[8]{0:T(128)S(1)}, u32[]{:S(2)}) copy-start(f32[8]{0:T(128)S(1)} %get-tuple-element.199) | copy-start | bytes 100
  314.6 1.7 copy-start.6
  314.6 3.0 copy-start.8
  319.3 276.1 %all-reduce.4.cloned.1.call-start = ((), (), s32[]{:S(2)}) async-start(), calls=%async_computation.4 | async-start | bytes 1048576 | tf_op jit(solution)/shard_map/psum | solution.py:102
  319.5 5.8 copy-start.7
Sparse Core Ops, SparseCore 0:
  10.6 151.3 all-gather.6
  176.3 117.6 all-gather.8
  319.4 113.8 all-gather.10
  440.5 154.8 all-reduce.3
